TPU v7x, 32 devices: a whole 2x2x4 slice. The times are simulated.
32 devices in a mesh: peer: 8 (over z, y), grp: 4 (over x, core).
Axes of the slice: x: 2, y: 2, z: 4, core: 2. Of those that a mesh axis runs over, the one named last changes fastest.
Arguments:
- tokens: bfloat16 [4096, 2048], P(('peer', 'grp')), may hold values from -6 to 6
- cotangent: bfloat16 [4096, 2048], P(('peer', 'grp')), may hold values from -6 to 6
- expert_ids: int32 [4096, 4], P(('peer', 'grp')), may hold values from 0 to 31, all different within a row; in each aligned block of 128 rows (0 to 127, 128 to 255, ...) at most 32 rows name the same one
- route_prob: float32 [4096, 4], P(('peer', 'grp')), may hold values from 0.1 to 1
- w_gate: bfloat16 [8, 2048, 704], P('peer', None, 'grp'), may hold values from -0.125 to 0.125
- w_up: bfloat16 [8, 2048, 704], P('peer', None, 'grp'), may hold values from -0.125 to 0.125
- w_down: bfloat16 [8, 704, 2048], P('peer', 'grp'), may hold values from -0.21875 to 0.21875
- student_logits: bfloat16 [8, 8, 151936], P('peer', None, 'grp'), may hold values from -24 to 252
- stale_logits: bfloat16 [8, 8, 151936], P('peer', None, 'grp'), may hold values from -24 to 252
- labels: int32 [8, 8], P('peer'), may hold values from 0 to 151935
Outputs:
- layer_out: bfloat16 [4096, 2048], P(('peer', 'grp'))
- input_grad: bfloat16 [4096, 2048], P(('peer', 'grp'))
- prob_grad: float32 [4096, 4], P(('peer', 'grp'))
- distill_loss: float32 [8, 8], P('peer')
- logit_grad: bfloat16 [8, 8, 151936], P('peer', None, 'grp')
Inputs may be any that keep to these rules, and one draw needn't show every extreme that they name: `expert_ids`: each row names 4 different experts; the rows of one device name any one expert at most 32 times.
All inputs are finite; a program needn't handle non-finite values.
Results may differ from a plain program's by a relative error of at most 0.0064.
Values may be sent and summed in bfloat16 or wider, within the bound.
No kernel may reach another device: no remote copies, remote signals or barrier semaphores. Data moves between devices by JAX's collectives and lax.ppermute only.
A program may use at most 64 MiB of HBM per device.

v0:
```python
import jax
import jax.numpy as jnp
from jax import lax
from jax.sharding import PartitionSpec as P

PIECES = 4
CAP = 32


def joined(value, axis, combine):
    everything = jax.tree.map(lambda part: lax.all_gather(part, axis), value)
    leading = jax.tree.map(lambda part: part[0], everything)

    def lap(k, so_far):
        return combine(so_far, jax.tree.map(lambda part: part[k], everything))

    return lax.fori_loop(1, lax.axis_size(axis), lap, leading)


def from_behind(value, axis, steps):
    count = lax.axis_size(axis)
    pairs = [(source, (source + steps) % count) for source in range(count)]
    return lax.ppermute(value, axis, pairs)


def slot_tables(expert_ids, n_window, capacity):
    window_iota = lax.broadcasted_iota(jnp.int32, (1, 1, n_window), 2)
    member = jnp.sum((expert_ids[:, :, None] == window_iota).astype(jnp.int32), axis=1)
    position = jnp.cumsum(member, axis=0) - member
    slot_iota = lax.broadcasted_iota(jnp.int32, (1, capacity, 1), 1)
    select = (position.T[:, None, :] == slot_iota) & (member.T[:, None, :] > 0)
    return (position, select)


def forward_piece(slot_rows, gate_cols, up_cols, down_rows):
    gate_act = jnp.dot(slot_rows, gate_cols, preferred_element_type=jnp.float32)
    up_act = jnp.dot(slot_rows, up_cols, preferred_element_type=jnp.float32)
    hidden = (gate_act * jax.nn.sigmoid(gate_act) * up_act).astype(jnp.bfloat16)
    piece_out = jnp.dot(hidden, down_rows, preferred_element_type=jnp.float32).astype(jnp.bfloat16)
    return (piece_out, gate_act, up_act)


def backward_piece(scaled_rows, gate_act, up_act, gate_cols, up_cols, down_rows):
    contract = (((1,), (1,)), ((), ()))
    grad_hidden = lax.dot_general(
        scaled_rows, down_rows, contract, preferred_element_type=jnp.float32
    )
    sigmoid_gate = jax.nn.sigmoid(gate_act)
    grad_gate = (
        grad_hidden * up_act * sigmoid_gate * (1.0 + gate_act * (1.0 - sigmoid_gate))
    ).astype(jnp.bfloat16)
    grad_up = (grad_hidden * gate_act * sigmoid_gate).astype(jnp.bfloat16)
    piece_grad = lax.dot_general(grad_gate, gate_cols, contract, preferred_element_type=jnp.float32)
    piece_grad = piece_grad + lax.dot_general(
        grad_up, up_cols, contract, preferred_element_type=jnp.float32
    )
    return piece_grad.astype(jnp.bfloat16)


def join_stats(first_side, second_side):
    max_one, sum_one, tmax_one, tsum_one, cross_one, label_one = first_side
    max_two, sum_two, tmax_two, tsum_two, cross_two, label_two = second_side
    max_both = jnp.maximum(max_one, max_two)
    tmax_both = jnp.maximum(tmax_one, tmax_two)
    scale_one = jnp.exp(tmax_one - tmax_both)
    scale_two = jnp.exp(tmax_two - tmax_both)
    sum_both = sum_one * jnp.exp(max_one - max_both) + sum_two * jnp.exp(max_two - max_both)
    tsum_both = tsum_one * scale_one + tsum_two * scale_two
    cross_both = cross_one * scale_one + cross_two * scale_two
    return (max_both, sum_both, tmax_both, tsum_both, cross_both, label_one + label_two)


def distill(student_logits, teacher_now, labels):
    student = student_logits[0].astype(jnp.float32)
    teacher = teacher_now[0].astype(jnp.float32)
    shard_width = student.shape[1]
    vocab_ids = lax.axis_index("grp") * shard_width + lax.broadcasted_iota(
        jnp.int32, student.shape, 1
    )
    label_hit = vocab_ids == labels[0][:, None]
    label_logit = jnp.sum(jnp.where(label_hit, student, 0.0), axis=1)
    local_smax = jnp.max(student, axis=1)
    local_tmax = jnp.max(teacher, axis=1)
    student_exp = jnp.sum(jnp.exp(student - local_smax[:, None]), axis=1)
    teacher_exp = jnp.exp(teacher - local_tmax[:, None])
    teacher_sum = jnp.sum(teacher_exp, axis=1)
    cross_sum = jnp.sum(teacher_exp * (teacher - student), axis=1)
    max_student, student_sum, max_teacher, teacher_sum, cross_sum, label_logit = joined(
        (local_smax, student_exp, local_tmax, teacher_sum, cross_sum, label_logit),
        "grp",
        join_stats,
    )
    lse_student = max_student + jnp.log(student_sum)
    lse_teacher = max_teacher + jnp.log(teacher_sum)
    distill_loss = 2.0 * lse_student - label_logit + cross_sum / teacher_sum - lse_teacher
    teacher_prob = jnp.exp(teacher - lse_teacher[:, None])
    logit_grad = (
        2.0 * jnp.exp(student - lse_student[:, None]) - label_hit.astype(jnp.float32) - teacher_prob
    ).astype(jnp.bfloat16)
    return (distill_loss[None], logit_grad[None])


def body(
    tokens,
    cotangent,
    expert_ids,
    route_prob,
    w_gate,
    w_up,
    w_down,
    student_logits,
    stale_logits,
    labels,
):
    group_size = lax.axis_size("grp")
    n_window = group_size // PIECES
    gate_cols = w_gate[0]
    up_cols = w_up[0]
    down_rows = w_down[0]
    model_width = tokens.shape[1]
    half_cap = CAP // 2
    position, select = slot_tables(expert_ids, n_window, CAP)
    select_bf = select.astype(jnp.bfloat16)
    window_iota = lax.broadcasted_iota(jnp.int32, (1, 1, n_window), 2)
    token_prob = jnp.sum(
        route_prob[:, :, None] * (expert_ids[:, :, None] == window_iota).astype(jnp.float32), axis=1
    )
    slot_prob = jnp.einsum(
        "ect,te->ec", select.astype(jnp.float32), token_prob, precision=lax.Precision.HIGHEST
    )
    slot_rows = jnp.einsum(
        "ect,td->ecd", select_bf, tokens, preferred_element_type=jnp.float32
    ).astype(jnp.bfloat16)
    slot_cot = jnp.einsum("ect,td->ecd", select_bf, cotangent, preferred_element_type=jnp.float32)
    slot_scaled = (slot_prob[:, :, None] * slot_cot).astype(jnp.bfloat16)
    send_rows = jnp.repeat(slot_rows, PIECES, axis=0).reshape(group_size, 2, half_cap, model_width)
    send_scaled = jnp.repeat(slot_scaled, PIECES, axis=0).reshape(
        group_size, 2, half_cap, model_width
    )
    recv_rows = lax.all_to_all(send_rows, "grp", split_axis=0, concat_axis=0, tiled=True)
    recv_scaled = lax.all_to_all(send_scaled, "grp", split_axis=0, concat_axis=0, tiled=True)
    item_count = recv_rows.shape[1]
    flat_rows = recv_rows.reshape(-1, model_width)
    flat_scaled = recv_scaled.reshape(-1, model_width)
    piece_out, gate_act, up_act = forward_piece(flat_rows, gate_cols, up_cols, down_rows)
    piece_out = piece_out.reshape(group_size, item_count, half_cap, model_width)
    piece_grad = backward_piece(flat_scaled, gate_act, up_act, gate_cols, up_cols, down_rows)
    piece_grad = piece_grad.reshape(group_size, item_count, half_cap, model_width)
    back_out = lax.all_to_all(piece_out, "grp", split_axis=0, concat_axis=0, tiled=True)
    back_grad = lax.all_to_all(piece_grad, "grp", split_axis=0, concat_axis=0, tiled=True)
    back_out, back_grad = (back_out, back_grad)
    expert_out = jnp.sum(
        back_out.astype(jnp.float32).reshape(n_window, PIECES, CAP, model_width), axis=1
    )
    expert_grad = jnp.sum(
        back_grad.astype(jnp.float32).reshape(n_window, PIECES, CAP, model_width), axis=1
    )
    in_window = expert_ids < n_window
    safe_ids = jnp.where(in_window, expert_ids, 0)
    slot_index = jnp.take_along_axis(position, safe_ids, axis=1)
    flat_index = safe_ids * CAP + slot_index
    out_rows = jnp.where(
        in_window[:, :, None],
        jnp.take(expert_out.reshape(-1, model_width), flat_index, axis=0),
        0.0,
    )
    grad_rows = jnp.where(
        in_window[:, :, None],
        jnp.take(expert_grad.reshape(-1, model_width), flat_index, axis=0),
        0.0,
    )
    layer_out = jnp.sum(route_prob[:, :, None] * out_rows, axis=1).astype(jnp.bfloat16)
    prob_grad = jnp.sum(cotangent.astype(jnp.float32)[:, None, :] * out_rows, axis=2)
    input_grad = jnp.sum(grad_rows, axis=1).astype(jnp.bfloat16)
    teacher_now = from_behind(stale_logits, "peer", 1)
    distill_loss, logit_grad = distill(student_logits, teacher_now, labels)
    return (layer_out, input_grad, prob_grad, distill_loss, logit_grad)


def solution(mesh):
    placed = (
        P(("peer", "grp"), None),
        P(("peer", "grp"), None),
        P(("peer", "grp"), None),
        P(("peer", "grp"), None),
        P("peer", None, "grp"),
        P("peer", None, "grp"),
        P("peer", "grp", None),
        P("peer", None, "grp"),
        P("peer", None, "grp"),
        P("peer", None),
    )
    return jax.shard_map(
        body,
        mesh=mesh,
        in_specs=placed,
        out_specs=(
            P(("peer", "grp"), None),
            P(("peer", "grp"), None),
            P(("peer", "grp"), None),
            P("peer", None),
            P("peer", None, "grp"),
        ),
        check_vma=False,
    )
```

profile of v0, /device:TPU:0, one launch (start us, length us, event | category | flops | bytes accessed | tf_op | source)
XLA Modules:
  0.0 88.1 jit_solution(13793682521302028346)
XLA Ops:
  0.6 3.0 %collective-permute-start = (bf16[1,8,37984]{2,1,0:T(8,128)(2,1)}, bf16[1,8,37984]{2,1,0:T(8,128)(2,1)S(1)}, u32[]{:S(2)}, u32[]{:S(2)}) collective-permute-start(bf16[1,8,37984]{2,1,0:T(8,128)(2,1)} %param.22), channel_id=1, source_target_pairs={{0,4},{4,8},{8,12},{12,16},{16,20},{20,24},{24,28},{28,0},{1,5},{5... | collective-permute-start | bytes 1823240 | tf_op jit(solution)/shard_map/ppermute | solution.py:23
  4.9 1.2 %convolution_convert_fusion.1 = bf16[32,2048]{1,0:T(8,128)(2,1)S(1)} fusion(bf16[128,2048]{1,0:T(8,128)(2,1)} %param.14, s32[128]{0:T(128)S(1)} %sub.111, pred[128]{0:T(512)(128)(4,1)S(1)} %broadcast_compare_fusion.2), kind=kOutput, calls=%fused_computation.36 | convolution fusion | flops 16850944 | bytes 656000 | tf_op jit(solution)/shard_map/ect,td->ecd/dot_general | solution.py:131
  6.1 0.8 broadcast_in_dim.63
  7.0 3.5 %all-to-all-start = ((bf16[4,2,16,2048]{3,2,1,0:T(8,128)(2,1)}), bf16[4,2,16,2048]{3,2,1,0:T(8,128)(2,1)S(1)}, u32[]{:S(2)}, u32[]{:S(2)}) async-start(bf16[4,2,16,2048]{3,2,1,0:T(8,128)(2,1)} %broadcast_in_dim.63), calls=%async_computation | async-start | bytes 1048576 | tf_op jit(solution)/shard_map/all_to_all | solution.py:140
  10.8 3.4 %gather_fusion = s32[512]{0:T(512)S(1)} fusion(s32[128,1]{1,0:T(8,128)S(1)} %get-tuple-element.386, s32[512]{0:T(512)S(1)} %reshape.285), kind=kCustom, calls=%fused_computation.2 | custom fusion | bytes 8192 | tf_op jit(solution)/shard_map/jit(take_along_axis)/gather | solution.py:160
  16.4 0.7 copy.40
  17.5 1.2 %convert_element_type.89 = f32[128,2048]{1,0:T(8,128)} convert(bf16[128,2048]{1,0:T(8,128)(2,1)S(1)} %copy-done.5) | non-fusion elementwise | flops 262144 | bytes 1572864 | tf_op jit(solution)/shard_map/convert_element_type | solution.py:173
  19.2 0.8 broadcast_in_dim.67
  20.1 4.3 %all-to-all-start.2 = ((bf16[4,2,16,2048]{3,2,1,0:T(8,128)(2,1)}), bf16[4,2,16,2048]{3,2,1,0:T(8,128)(2,1)}, u32[]{:S(2)}, u32[]{:S(2)}) async-start(bf16[4,2,16,2048]{3,2,1,0:T(8,128)(2,1)} %broadcast_in_dim.67), calls=%async_computation.2 | async-start | bytes 1048576 | tf_op jit(solution)/shard_map/all_to_all | solution.py:141
  24.7 1.0 %fusion.39 = f32[128,176]{0,1:T(8,128)} fusion(bf16[128,2048]{1,0:T(8,128)(2,1)S(1)} %bitcast.127, bf16[1,2048,176]{1,2,0:T(8,128)(2,1)S(1)} %copy-done.3), kind=kOutput, calls=%fused_computation.65 | convolution fusion | flops 92274688 | bytes 1335296 | tf_op jit(solution)/shard_map/dot_general | solution.py:37
  25.8 7.4 %all-to-all-done.2 = bf16[4,2,16,2048]{3,2,1,0:T(8,128)(2,1)} async-done(((bf16[4,2,16,2048]{3,2,1,0:T(8,128)(2,1)}), bf16[4,2,16,2048]{3,2,1,0:T(8,128)(2,1)}, u32[]{:S(2)}, u32[]{:S(2)}) %all-to-all-start.2) | async-done | bytes 524320 | tf_op jit(solution)/shard_map/all_to_all | solution.py:141
  33.2 1.6 %fusion.35 = f32[128,176]{0,1:T(8,128)S(1)} fusion(bf16[128,2048]{1,0:T(8,128)(2,1)} %bitcast.18, bf16[1,176,2048]{2,1,0:T(8,128)(2,1)} %param.20), kind=kOutput, calls=%fused_computation.61 | convolution fusion | flops 92274688 | bytes 1335296 | tf_op jit(solution)/shard_map/dot_general | solution.py:45
  35.2 1.1 %fusion.16 = bf16[128,2048]{1,0:T(8,128)(2,1)} fusion(f32[128,2048]{1,0:T(8,128)S(1)} %fusion.41, bf16[1,2048,176]{1,2,0:T(8,128)(2,1)S(1)} %copy-done.3, f32[128,176]{0,1:T(8,128)S(1)} %fusion.35, f32[128,176]{0,1:T(8,128)S(1)} %fusion.43), kind=kOutput, calls=%fused_computation.32 | convolution fusion | flops 92934144 | bytes 2473984 | tf_op jit(solution)/shard_map/dot_general | solution.py:54
  36.4 3.6 %all-to-all-start.3 = ((bf16[4,2,16,2048]{3,2,1,0:T(8,128)(2,1)}), bf16[4,2,16,2048]{3,2,1,0:T(8,128)(2,1)S(1)}, u32[]{:S(2)}, u32[]{:S(2)}) async-start(bf16[4,2,16,2048]{3,2,1,0:T(8,128)(2,1)} %bitcast.19), calls=%async_computation.3 | async-start | bytes 1048576 | tf_op jit(solution)/shard_map/all_to_all | solution.py:150
  40.0 2.0 %convolution_convert_fusion = bf16[128,2048]{1,0:T(8,128)(2,1)} fusion(bf16[1,176,2048]{2,1,0:T(8,128)(2,1)S(1)} %copy-done.4, f32[128,176]{0,1:T(8,128)} %fusion.39, f32[128,176]{0,1:T(8,128)S(1)} %fusion.43), kind=kOutput, calls=%fused_computation.33 | convolution fusion | flops 92672000 | bytes 1425408 | tf_op jit(solution)/shard_map/dot_general | solution.py:39
  42.6 1.2 %fusion.33 = (f32[8]{0:T(128)S(1)}, f32[8]{0:T(128)S(1)}, f32[8]{0:T(128)S(1)}, f32[8]{0:T(128)S(1)}) fusion(bf16[1,8,37984]{2,1,0:T(8,128)(2,1)S(1)} %collective-permute-done, bf16[1,8,37984]{2,1,0:T(8,128)(2,1)S(1)} %copy-done.1, f32[8]{0:T(128)S(1)} %reduce_max.45, s32[8]{0:T(128)S(1)} %bitcast.137, s32[37984]{0:T(1024)S(1)} %iota_add_fusion, ...), kind=kLoop, calls=%fused_computation.56 | loop fusion | flops 3646432 | bytes 1367648 | tf_op jit(solution)/shard_map/reduce_sum | solution.py:87
  44.6 7.3 %all-reduce.6 = (f32[32]{0:T(128)S(1)}, f32[32]{0:T(128)S(1)}, f32[32]{0:T(128)S(1)}, f32[32]{0:T(128)S(1)}, f32[32]{0:T(128)S(1)}, /*index=5*/f32[32]{0:T(128)S(1)}) all-reduce(f32[32]{0:T(128)S(1)} %convert_dynamic-update-slice_fusion.1, f32[32]{0:T(128)S(1)} %dynamic-update-slice.1, ...), channel_id=2, replica_groups=mesh['peer'=8,'grp'=4] {'grp'}, use_global_device_ids=true, to_apply=%add | all-reduce | flops 192 | bytes 1536
  53.2 3.7 %all-to-all-start.1 = ((bf16[4,2,16,2048]{3,2,1,0:T(8,128)(2,1)}), bf16[4,2,16,2048]{3,2,1,0:T(8,128)(2,1)S(1)}, u32[]{:S(2)}, u32[]{:S(2)}) async-start(bf16[4,2,16,2048]{3,2,1,0:T(8,128)(2,1)} %bitcast.128), calls=%async_computation.1 | async-start | bytes 1048576 | tf_op jit(solution)/shard_map/all_to_all | solution.py:149
  56.9 1.4 %fusion.29 = bf16[1,8,37984]{2,1,0:T(8,128)(2,1)} fusion(bf16[1,8,37984]{2,1,0:T(8,128)(2,1)S(1)} %copy-done.1, bf16[1,8,37984]{2,1,0:T(8,128)(2,1)S(1)} %collective-permute-done, f32[8]{0:T(128)S(1)} %get-tuple-element.380, s32[37984]{0:T(1024)S(1)} %iota_add_fusion, f32[8]{0:T(128)S(1)} %get-tuple-element.379, s32[8]{0:T(128)S(1)} %bitcast.138), kind=kLoop, calls=%fused_computation.52 | loop fusion | flops 3038720 | bytes 1975264 | tf_op jit(solution)/shard_map/convert_element_type | solution.py:99
  58.4 3.6 %gather_fusion.2 = f32[512,2048]{1,0:T(8,128)} fusion(f32[32,2048]{1,0:T(8,128)S(1)} %bitcast.125, s32[1024]{0:T(1024)S(1)} %pad_clamp_fusion), kind=kCustom, calls=%fused_computation.1.clone | custom fusion | bytes 8390656 | tf_op jit(solution)/shard_map/jit(_take)/gather | solution.py:169
  62.0 5.2 %reshape.355 = f32[128,4,2048]{2,1,0:T(4,128)} reshape(f32[512,2048]{1,0:T(8,128)} %gather_fusion.2) | data formatting | bytes 8388608 | tf_op jit(solution)/shard_map/jit(_take)/gather | solution.py:169
  67.3 3.6 %gather_fusion.1 = f32[512,2048]{1,0:T(8,128)} fusion(f32[32,2048]{1,0:T(8,128)S(1)} %bitcast.124, s32[1024]{0:T(1024)S(1)} %pad_clamp_fusion), kind=kCustom, calls=%fused_computation.clone | custom fusion | bytes 8390656 | tf_op jit(solution)/shard_map/jit(_take)/gather | solution.py:164
  70.9 5.3 %reshape.351 = f32[128,4,2048]{2,1,0:T(4,128)} reshape(f32[512,2048]{1,0:T(8,128)} %gather_fusion.1) | data formatting | bytes 8388608 | tf_op jit(solution)/shard_map/jit(_take)/gather | solution.py:164
  76.1 11.4 %multiply_reduce_fusion = (f32[128,4]{1,0:T(8,128)S(1)}, bf16[128,2048]{1,0:T(8,128)(2,1)}, bf16[128,2048]{1,0:T(8,128)(2,1)}) fusion(f32[128,4,2048]{2,1,0:T(4,128)} %reshape.351, f32[128,2048]{1,0:T(8,128)S(1)} %copy-done.2, pred[128,4]{1,0:T(8,128)(4,1)S(1)} %copy.46, pred[128,4]{1,0:T(8,128)(4,1)S(1)} %copy.41, f32[128,4]{1,0:T(8,128)S(1)} %copy-done.7, ...), kind=kLoop, calls=%fused_computation.29 | loop fusion | flops 8912384 | bytes 10490880 | tf_op jit(solution)/shard_map/reduce_sum | solution.py:173
  (91 shorter events, 8.3 us)
Async XLA Ops:
  0.6 23.7 %copy-start = (bf16[1,2048,176]{1,2,0:T(8,128)(2,1)S(1)}, bf16[1,2048,176]{1,2,0:T(8,128)(2,1)}, u32[]{:S(2)}) copy-start(bf16[1,2048,176]{1,2,0:T(8,128)(2,1)} %param.18) | copy-start | bytes 2162692
  0.6 41.4 %collective-permute-start = (bf16[1,8,37984]{2,1,0:T(8,128)(2,1)}, bf16[1,8,37984]{2,1,0:T(8,128)(2,1)S(1)}, u32[]{:S(2)}, u32[]{:S(2)}) collective-permute-start(bf16[1,8,37984]{2,1,0:T(8,128)(2,1)} %param.22), channel_id=1, source_target_pairs={{0,4},{4,8},{8,12},{12,16},{16,20},{20,24},{24,28},{28,0},{1,5},{5... | collective-permute-start | bytes 1823240 | tf_op jit(solution)/shard_map/ppermute | solution.py:23
  4.8 5.6 %copy-start.8 = (s32[128,4]{0,1:T(4,128)S(1)}, s32[128,4]{0,1:T(4,128)}, u32[]{:S(2)}) copy-start(s32[128,4]{0,1:T(4,128)} %param.16) | copy-start | bytes 6148
  7.0 12.3 %all-to-all-start = ((bf16[4,2,16,2048]{3,2,1,0:T(8,128)(2,1)}), bf16[4,2,16,2048]{3,2,1,0:T(8,128)(2,1)S(1)}, u32[]{:S(2)}, u32[]{:S(2)}) async-start(bf16[4,2,16,2048]{3,2,1,0:T(8,128)(2,1)} %broadcast_in_dim.63), calls=%async_computation | async-start | bytes 1048576 | tf_op jit(solution)/shard_map/all_to_all | solution.py:140
  10.7 3.9 %copy-start.1 = (bf16[1,8,37984]{2,1,0:T(8,128)(2,1)S(1)}, bf16[1,8,37984]{2,1,0:T(8,128)(2,1)}, u32[]{:S(2)}) copy-start(bf16[1,8,37984]{2,1,0:T(8,128)(2,1)} %param.21) | copy-start | bytes 1823236
  10.7 4.3 %copy-start.11 = (u32[32]{0:T(128)S(1)}, u32[32]{0:T(128)}, u32[]{:S(2)}) copy-start(u32[32]{0:T(128)} %constant.107) | copy-start | bytes 388
  10.7 5.7 %copy-start.9 = (f32[128,4]{0,1:T(4,128)S(1)}, f32[128,4]{0,1:T(4,128)}, u32[]{:S(2)}) copy-start(f32[128,4]{0,1:T(4,128)} %param.17) | copy-start | bytes 6148
  14.2 3.3 %copy-start.5 = (bf16[128,2048]{1,0:T(8,128)(2,1)S(1)}, bf16[128,2048]{1,0:T(8,128)(2,1)}, u32[]{:S(2)}) copy-start(bf16[128,2048]{1,0:T(8,128)(2,1)} %param.15) | copy-start | bytes 1572868
  20.1 4.7 %copy-start.3 = (bf16[1,2048,176]{1,2,0:T(8,128)(2,1)S(1)}, bf16[1,2048,176]{1,2,0:T(8,128)(2,1)}, u32[]{:S(2)}) copy-start(bf16[1,2048,176]{1,2,0:T(8,128)(2,1)} %param.19) | copy-start | bytes 2162692
  20.1 13.1 %all-to-all-start.2 = ((bf16[4,2,16,2048]{3,2,1,0:T(8,128)(2,1)}), bf16[4,2,16,2048]{3,2,1,0:T(8,128)(2,1)}, u32[]{:S(2)}, u32[]{:S(2)}) async-start(bf16[4,2,16,2048]{3,2,1,0:T(8,128)(2,1)} %broadcast_in_dim.67), calls=%async_computation.2 | async-start | bytes 1048576 | tf_op jit(solution)/shard_map/all_to_all | solution.py:141
  25.8 9.1 %copy-start.6 = (f32[128,176]{0,1:T(8,128)S(1)}, f32[128,176]{0,1:T(8,128)}, u32[]{:S(2)}) copy-start(f32[128,176]{0,1:T(8,128)} %fusion.39) | copy-start | bytes 270340
  36.4 3.6 %copy-start.4 = (bf16[1,176,2048]{2,1,0:T(8,128)(2,1)S(1)}, bf16[1,176,2048]{2,1,0:T(8,128)(2,1)}, u32[]{:S(2)}) copy-start(bf16[1,176,2048]{2,1,0:T(8,128)(2,1)} %param.20) | copy-start | bytes 2162692
  36.4 16.9 %all-to-all-start.3 = ((bf16[4,2,16,2048]{3,2,1,0:T(8,128)(2,1)}), bf16[4,2,16,2048]{3,2,1,0:T(8,128)(2,1)S(1)}, u32[]{:S(2)}, u32[]{:S(2)}) async-start(bf16[4,2,16,2048]{3,2,1,0:T(8,128)(2,1)} %bitcast.19), calls=%async_computation.3 | async-start | bytes 1048576 | tf_op jit(solution)/shard_map/all_to_all | solution.py:150
  40.0 2.6 %copy-start.10 = (s32[1,8]{1,0:T(1,128)S(1)}, s32[1,8]{1,0:T(1,128)}, u32[]{:S(2)}) copy-start(s32[1,8]{1,0:T(1,128)} %param.23) | copy-start | bytes 100
  53.2 14.0 %all-to-all-start.1 = ((bf16[4,2,16,2048]{3,2,1,0:T(8,128)(2,1)}), bf16[4,2,16,2048]{3,2,1,0:T(8,128)(2,1)S(1)}, u32[]{:S(2)}, u32[]{:S(2)}) async-start(bf16[4,2,16,2048]{3,2,1,0:T(8,128)(2,1)} %bitcast.128), calls=%async_computation.1 | async-start | bytes 1048576 | tf_op jit(solution)/shard_map/all_to_all | solution.py:149
  70.9 5.3 %copy-start.2 = (f32[128,2048]{1,0:T(8,128)S(1)}, f32[128,2048]{1,0:T(8,128)}, u32[]{:S(2)}) copy-start(f32[128,2048]{1,0:T(8,128)} %convert_element_type.89) | copy-start | bytes 3145732
  70.9 5.3 %copy-start.7 = (f32[128,4]{1,0:T(8,128)S(1)}, f32[128,4]{1,0:T(8,128)}, u32[]{:S(2)}) copy-start(f32[128,4]{1,0:T(8,128)} %copy.40) | copy-start | bytes 6148
where the time goes:
time: 88.8 us; the launch traced here: 88.1 us
  local copies, waits for them, and re-layouts  27.1 us (31%)
  other arithmetic  18.1 us (20%)
  starting transfers between devices  18 us (20%)
  matrix products  8.18 us (9%)
  waiting for transfers between devices  7.67 us (9%)
  blocking collectives  7.33 us (8%)
  between operations  1.6 us (2%)
    reduce_sum x1, other arithmetic, body(): jnp.sum(cotangent.astype(jnp.float32)[:, None, :] * out_rows, axis=2)  11.4 us
    gather x2, local copies, waits for them, and re-layouts, body(): jnp.take(expert_out.reshape(-1, model_width), flat_index, axis=0)  8.83 us
    gather x2, local copies, waits for them, and re-layouts, body(): jnp.take(expert_grad.reshape(-1, model_width), flat_index, axis=0)  8.79 us
    all_to_all x1, waiting for transfers between devices, body(): lax.all_to_all(send_scaled, 'grp', split_axis=0, concat_axis=0, tiled=True)  7.41 us
    unnamed x1, blocking collectives  7.33 us
    all_to_all x1, starting transfers between devices, body(): lax.all_to_all(send_scaled, 'grp', split_axis=0, concat_axis=0, tiled=True)  4.26 us
    gather x5, local copies, waits for them, and re-layouts, body(): slot_index = jnp.take_along_axis(position, safe_ids, axis=1)  3.81 us
    all_to_all x1, starting transfers between devices, body(): lax.all_to_all(piece_out, 'grp', split_axis=0, concat_axis=0, tiled=True)  3.65 us
  transfers between devices with their start and end apart: 5, of which 2 were waited for; matrix products, arithmetic and copies ran while one was open for 37% of the time, Pallas kernels for 0%

commit v1 on v0

--- a/solution.py
+++ b/solution.py
@@ -5,6 +5,17 @@
 
 PIECES = 4
 CAP = 32
+
+
+def split_up(x, dim, size):
+    before, after = (x.shape[:dim], x.shape[dim + 1 :])
+    return jnp.moveaxis(x.reshape(*before, size, -1, *after), dim, 0)
+
+
+def laid_out(parts, dim):
+    parts = jnp.moveaxis(parts, 0, dim)
+    shape = parts.shape
+    return parts.reshape(*shape[:dim], shape[dim] * shape[dim + 1], *shape[dim + 2 :])
 
 
 def joined(value, axis, combine):
@@ -138,7 +149,15 @@
         group_size, 2, half_cap, model_width
     )
     recv_rows = lax.all_to_all(send_rows, "grp", split_axis=0, concat_axis=0, tiled=True)
-    recv_scaled = lax.all_to_all(send_scaled, "grp", split_axis=0, concat_axis=0, tiled=True)
+    size, index = (lax.axis_size("grp"), lax.axis_index("grp"))
+    blocks = split_up(send_scaled, 0, size)
+    out = blocks
+    for step in range(1, size):
+        target, source_2 = ((index + step) % size, (index - step) % size)
+        sent = lax.dynamic_index_in_dim(blocks, target, 0)
+        received = lax.ppermute(sent, "grp", [(i, (i + step) % size) for i in range(size)])
+        out = lax.dynamic_update_slice_in_dim(out, received, source_2, axis=0)
+    recv_scaled = laid_out(out, 0)
     item_count = recv_rows.shape[1]
     flat_rows = recv_rows.reshape(-1, model_width)
     flat_scaled = recv_scaled.reshape(-1, model_width)

time: 88.8 us -> 82.5 us (0.929)
  waiting for transfers between devices: 7.67 us -> 0.02 us
  local copies, waits for them, and re-layouts: 27.1 us -> 29.7 us
  starting transfers between devices: 18 us -> 16.7 us
    all_to_all x1 -> x0, waiting for transfers between devices: 7.41 us -> none  [body(): lax.all_to_all(send_scaled, 'grp', split_axis=0, concat_axis=0, tiled=True)]
    ppermute x0 -> x3, starting transfers between devices: none -> 4.48 us  [body(): lax.ppermute(sent, 'grp', [(i, (i + step) % size) for i in range(size)])]
    all_to_all x1 -> x0, starting transfers between devices: 4.26 us -> none  [body(): lax.all_to_all(send_scaled, 'grp', split_axis=0, concat_axis=0, tiled=True)]
    dynamic_update_slice x0 -> x3, local copies, waits for them, and re-layouts: none -> 2.76 us  [body(): out = lax.dynamic_update_slice_in_dim(out, received, source_2, axis=0)]
    ppermute x1, starting transfers between devices: 3.05 us -> 1.52 us  [from_behind(): return lax.ppermute(value, axis, pairs)]
    dot_general x1, matrix products: 1.24 us -> 0.19 us  [body(): jnp.einsum('ect,td->ecd', select_bf, tokens, preferred_element_type=jnp.f...]
    dot_general x1, matrix products: 0.22 us -> 1.27 us  [body(): jnp.einsum('ect,td->ecd', select_bf, cotangent, preferred_element_type=jn...]
    unnamed x37 -> x41, local copies, waits for them, and re-layouts: 2.89 us -> 3.53 us
  transfers between devices with their start and end apart: 5 -> 7, of which waited for: 2 -> 0; matrix products, arithmetic and copies ran while one was open for 37% -> 39% of each run, Pallas kernels for 0% -> 0%
where the time goes in v1:
time: 82.5 us; the launch traced here: 81.9 us
  local copies, waits for them, and re-layouts  29.7 us (36%)
  other arithmetic  18.2 us (22%)
  starting transfers between devices  16.7 us (20%)
  matrix products  8.07 us (10%)
  blocking collectives  7.34 us (9%)
  between operations  1.67 us (2%)
    reduce_sum x1, other arithmetic, body(): jnp.sum(cotangent.astype(jnp.float32)[:, None, :] * out_rows, axis=2)  11.4 us
    gather x2, local copies, waits for them, and re-layouts, body(): jnp.take(expert_out.reshape(-1, model_width), flat_index, axis=0)  8.83 us
    gather x2, local copies, waits for them, and re-layouts, body(): jnp.take(expert_grad.reshape(-1, model_width), flat_index, axis=0)  8.79 us
    unnamed x1, blocking collectives  7.34 us
    ppermute x3, starting transfers between devices, body(): lax.ppermute(sent, 'grp', [(i, (i + step) % size) for i in range(size)])  4.48 us
    gather x5, local copies, waits for them, and re-layouts, body(): slot_index = jnp.take_along_axis(position, safe_ids, axis=1)  3.81 us
    all_to_all x1, starting transfers between devices, body(): lax.all_to_all(piece_out, 'grp', split_axis=0, concat_axis=0, tiled=True)  3.65 us
    all_to_all x1, starting transfers between devices, body(): lax.all_to_all(piece_grad, 'grp', split_axis=0, concat_axis=0, tiled=True)  3.6 us
  transfers between devices with their start and end apart: 7, of which 0 were waited for; matrix products, arithmetic and copies ran while one was open for 39% of the time, Pallas kernels for 0%

profile of v1, /device:TPU:0, one launch (start us, length us, event | category | flops | bytes accessed | tf_op | source)
XLA Modules:
  0.0 81.9 jit_solution(8830657055690544281)
XLA Ops:
  2.0 1.3 %fusion.17 = bf16[32,2048]{1,0:T(8,128)(2,1)S(1)} fusion(bf16[128,2048]{1,0:T(8,128)(2,1)} %param.15, f32[32]{0:T(128)S(1)} %convolution_bitcast_fusion, s32[128]{0:T(128)S(1)} %sub.120, pred[128]{0:T(512)(128)(4,1)S(1)} %broadcast_compare_fusion.2), kind=kOutput, calls=%fused_computation.35 | convolution fusion | flops 16916480 | bytes 656128 | tf_op jit(solution)/shard_map/ect,td->ecd/dot_general | solution.py:145
  3.9 2.6 %collective-permute-start.1 = (bf16[1,1,2,16,2048]{4,3,2,1,0:T(8,128)(2,1)S(1)}, bf16[1,1,2,16,2048]{4,3,2,1,0:T(8,128)(2,1)}, u32[]{:S(2)}, u32[]{:S(2)}) collective-permute-start(bf16[1,1,2,16,2048]{4,3,2,1,0:T(8,128)(2,1)S(1)} %bitcast.133), channel_id=1, source_target_pairs={{0,2},{1,3},{2,0},{3,1},{4,6},{5,7},{6,4},{7,5},{8,10},{9,11},{10,... | collective-permute-start | bytes 393224 | tf_op jit(solution)/shard_map/ppermute | solution.py:158
  6.4 1.4 %collective-permute-start.2 = (bf16[1,1,2,16,2048]{4,3,2,1,0:T(8,128)(2,1)S(1)}, bf16[1,1,2,16,2048]{4,3,2,1,0:T(8,128)(2,1)}, u32[]{:S(2)}, u32[]{:S(2)}) collective-permute-start(bf16[1,1,2,16,2048]{4,3,2,1,0:T(8,128)(2,1)S(1)} %bitcast.134), channel_id=1, source_target_pairs={{0,3},{1,0},{2,1},{3,2},{4,7},{5,4},{6,5},{7,6},{8,11},{9,8},{10,9... | collective-permute-start | bytes 393224 | tf_op jit(solution)/shard_map/ppermute | solution.py:158
  7.8 1.5 %collective-permute-start.3 = (bf16[1,8,37984]{2,1,0:T(8,128)(2,1)}, bf16[1,8,37984]{2,1,0:T(8,128)(2,1)S(1)}, u32[]{:S(2)}, u32[]{:S(2)}) collective-permute-start(bf16[1,8,37984]{2,1,0:T(8,128)(2,1)} %param.22), channel_id=1, source_target_pairs={{0,4},{4,8},{8,12},{12,16},{16,20},{20,24},{24,28},{28,0},{1,5},{5... | collective-permute-start | bytes 1823240 | tf_op jit(solution)/shard_map/ppermute | solution.py:34
  9.5 0.9 %broadcast_in_dim.65 = bf16[4,2,16,2048]{3,2,1,0:T(8,128)(2,1)} broadcast(bf16[2,16,2048]{2,1,0:T(8,128)(2,1)S(1)} %bitcast.131), dimensions={1,2,3} | broadcast | bytes 655360 | tf_op jit(solution)/shard_map/broadcast_in_dim | solution.py:147
  10.4 3.5 %all-to-all-start = ((bf16[4,2,16,2048]{3,2,1,0:T(8,128)(2,1)}), bf16[4,2,16,2048]{3,2,1,0:T(8,128)(2,1)S(1)}, u32[]{:S(2)}, u32[]{:S(2)}) async-start(bf16[4,2,16,2048]{3,2,1,0:T(8,128)(2,1)} %broadcast_in_dim.65), calls=%async_computation | async-start | bytes 1048576 | tf_op jit(solution)/shard_map/all_to_all | solution.py:151
  14.2 3.4 %gather_fusion = s32[512]{0:T(512)S(1)} fusion(s32[128,1]{1,0:T(8,128)S(1)} %get-tuple-element.386, s32[512]{0:T(512)S(1)} %reshape.287), kind=kCustom, calls=%fused_computation.2 | custom fusion | bytes 8192 | tf_op jit(solution)/shard_map/jit(take_along_axis)/gather | solution.py:179
  19.6 1.2 %convert_element_type.89 = f32[128,2048]{1,0:T(8,128)} convert(bf16[128,2048]{1,0:T(8,128)(2,1)S(1)} %copy-done.5) | non-fusion elementwise | flops 262144 | bytes 1572864 | tf_op jit(solution)/shard_map/convert_element_type | solution.py:192
  22.1 0.9 %constant_dynamic-update-slice_fusion.2 = bf16[4,1,2,16,2048]{4,3,2,1,0:T(8,128)(2,1)S(1)} fusion(bf16[4,1,2,16,2048]{4,3,2,1,0:T(8,128)(2,1)S(1)} %broadcast_in_dim.69, bf16[1,1,2,16,2048]{4,3,2,1,0:T(8,128)(2,1)} %collective-permute-done, s32[]{:T(128)S(6)} %select_n.84), kind=kLoop, calls=%fused_computation.98 | loop fusion | bytes 262148 | tf_op jit(solution)/shard_map/dynamic_update_slice | solution.py:159
  23.1 0.9 %constant_dynamic-update-slice_fusion.1 = bf16[4,1,2,16,2048]{4,3,2,1,0:T(8,128)(2,1)S(1)} fusion(bf16[4,1,2,16,2048]{4,3,2,1,0:T(8,128)(2,1)S(1)} %constant_dynamic-update-slice_fusion.2, bf16[1,1,2,16,2048]{4,3,2,1,0:T(8,128)(2,1)} %collective-permute-done.1, s32[]{:T(128)S(6)} %select_n.86), kind=kLoop, calls=%fused_computation.97 | loop fusion | bytes 262148 | tf_op jit(solution)/shard_map/dynamic_update_slice | solution.py:159
  24.0 0.9 %constant_dynamic-update-slice_fusion = bf16[4,1,2,16,2048]{4,3,2,1,0:T(8,128)(2,1)S(1)} fusion(bf16[4,1,2,16,2048]{4,3,2,1,0:T(8,128)(2,1)S(1)} %constant_dynamic-update-slice_fusion.1, bf16[1,1,2,16,2048]{4,3,2,1,0:T(8,128)(2,1)} %collective-permute-done.2, s32[]{:T(128)S(6)} %select_n.88), kind=kLoop, calls=%fused_computation.96 | loop fusion | bytes 262148 | tf_op jit(solution)/shard_map/dynamic_update_slice | solution.py:159
  24.9 2.2 %fusion.35 = f32[128,176]{0,1:T(8,128)} fusion(bf16[128,2048]{1,0:T(8,128)(2,1)S(1)} %bitcast.129, bf16[1,176,2048]{2,1,0:T(8,128)(2,1)} %param.20), kind=kOutput, calls=%fused_computation.61 | convolution fusion | flops 92274688 | bytes 1335296 | tf_op jit(solution)/shard_map/dot_general | solution.py:56
  28.9 1.1 %fusion.16 = bf16[128,2048]{1,0:T(8,128)(2,1)} fusion(f32[128,2048]{1,0:T(8,128)S(1)} %fusion.41, bf16[1,2048,176]{1,2,0:T(8,128)(2,1)S(1)} %copy-done.3, f32[128,176]{0,1:T(8,128)S(1)} %copy-done.6, f32[128,176]{0,1:T(8,128)S(1)} %fusion.43), kind=kOutput, calls=%fused_computation.32 | convolution fusion | flops 92934144 | bytes 2473984 | tf_op jit(solution)/shard_map/dot_general | solution.py:65
  30.1 3.6 %all-to-all-start.2 = ((bf16[4,2,16,2048]{3,2,1,0:T(8,128)(2,1)}), bf16[4,2,16,2048]{3,2,1,0:T(8,128)(2,1)S(1)}, u32[]{:S(2)}, u32[]{:S(2)}) async-start(bf16[4,2,16,2048]{3,2,1,0:T(8,128)(2,1)} %bitcast.20), calls=%async_computation.2 | async-start | bytes 1048576 | tf_op jit(solution)/shard_map/all_to_all | solution.py:169
  33.7 2.0 %convolution_convert_fusion = bf16[128,2048]{1,0:T(8,128)(2,1)} fusion(bf16[1,176,2048]{2,1,0:T(8,128)(2,1)S(1)} %copy-done.4, f32[128,176]{0,1:T(8,128)} %copy-done.7, f32[128,176]{0,1:T(8,128)S(1)} %fusion.43), kind=kOutput, calls=%fused_computation.33 | convolution fusion | flops 92672000 | bytes 1425408 | tf_op jit(solution)/shard_map/dot_general | solution.py:50
  36.3 1.2 %fusion.33 = (f32[8]{0:T(128)S(1)}, f32[8]{0:T(128)S(1)}, f32[8]{0:T(128)S(1)}, f32[8]{0:T(128)S(1)}) fusion(bf16[1,8,37984]{2,1,0:T(8,128)(2,1)S(1)} %collective-permute-done.3, bf16[1,8,37984]{2,1,0:T(8,128)(2,1)S(1)} %copy-done.1, f32[8]{0:T(128)S(1)} %reduce_max.45, s32[8]{0:T(128)S(1)} %bitcast.142, s32[37984]{0:T(1024)S(1)} %iota_add_fusion, ...), kind=kLoop, calls=%fused_computation.56 | loop fusion | flops 3646432 | bytes 1367648 | tf_op jit(solution)/shard_map/reduce_sum | solution.py:98
  38.3 7.3 %all-reduce.6 = (f32[32]{0:T(128)S(1)}, f32[32]{0:T(128)S(1)}, f32[32]{0:T(128)S(1)}, f32[32]{0:T(128)S(1)}, f32[32]{0:T(128)S(1)}, /*index=5*/f32[32]{0:T(128)S(1)}) all-reduce(f32[32]{0:T(128)S(1)} %convert_dynamic-update-slice_fusion.1, f32[32]{0:T(128)S(1)} %dynamic-update-slice.1, ...), channel_id=2, replica_groups=mesh['peer'=8,'grp'=4] {'grp'}, use_global_device_ids=true, to_apply=%add | all-reduce | flops 192 | bytes 1536
  47.0 3.7 %all-to-all-start.1 = ((bf16[4,2,16,2048]{3,2,1,0:T(8,128)(2,1)}), bf16[4,2,16,2048]{3,2,1,0:T(8,128)(2,1)S(1)}, u32[]{:S(2)}, u32[]{:S(2)}) async-start(bf16[4,2,16,2048]{3,2,1,0:T(8,128)(2,1)} %bitcast.130), calls=%async_computation.1 | async-start | bytes 1048576 | tf_op jit(solution)/shard_map/all_to_all | solution.py:168
  50.6 1.4 %fusion.29 = bf16[1,8,37984]{2,1,0:T(8,128)(2,1)} fusion(bf16[1,8,37984]{2,1,0:T(8,128)(2,1)S(1)} %copy-done.1, bf16[1,8,37984]{2,1,0:T(8,128)(2,1)S(1)} %collective-permute-done.3, f32[8]{0:T(128)S(1)} %get-tuple-element.380, s32[37984]{0:T(1024)S(1)} %iota_add_fusion, f32[8]{0:T(128)S(1)} %get-tuple-element.379, s32[8]{0:T(128)S(1)} %bitcast.143), kind=kLoop, calls=%fused_computation.52 | loop fusion | flops 3038720 | bytes 1975264 | tf_op jit(solution)/shard_map/convert_element_type | solution.py:110
  52.1 3.6 %gather_fusion.2 = f32[512,2048]{1,0:T(8,128)} fusion(f32[32,2048]{1,0:T(8,128)S(1)} %bitcast.126, s32[1024]{0:T(1024)S(1)} %pad_clamp_fusion), kind=kCustom, calls=%fused_computation.1.clone | custom fusion | bytes 8390656 | tf_op jit(solution)/shard_map/jit(_take)/gather | solution.py:188
  55.8 5.2 %reshape.357 = f32[128,4,2048]{2,1,0:T(4,128)} reshape(f32[512,2048]{1,0:T(8,128)} %gather_fusion.2) | data formatting | bytes 8388608 | tf_op jit(solution)/shard_map/jit(_take)/gather | solution.py:188
  61.0 3.6 %gather_fusion.1 = f32[512,2048]{1,0:T(8,128)} fusion(f32[32,2048]{1,0:T(8,128)S(1)} %bitcast.125, s32[1024]{0:T(1024)S(1)} %pad_clamp_fusion), kind=kCustom, calls=%fused_computation.clone | custom fusion | bytes 8390656 | tf_op jit(solution)/shard_map/jit(_take)/gather | solution.py:183
  64.6 5.3 %reshape.353 = f32[128,4,2048]{2,1,0:T(4,128)} reshape(f32[512,2048]{1,0:T(8,128)} %gather_fusion.1) | data formatting | bytes 8388608 | tf_op jit(solution)/shard_map/jit(_take)/gather | solution.py:183
  69.8 11.4 %multiply_reduce_fusion = (f32[128,4]{1,0:T(8,128)S(1)}, bf16[128,2048]{1,0:T(8,128)(2,1)}, bf16[128,2048]{1,0:T(8,128)(2,1)}) fusion(f32[128,4,2048]{2,1,0:T(4,128)} %reshape.353, f32[128,2048]{1,0:T(8,128)S(1)} %copy-done.2, pred[128,4]{1,0:T(8,128)(4,1)S(1)} %copy.46, pred[128,4]{1,0:T(8,128)(4,1)S(1)} %copy.41, f32[128,4]{1,0:T(8,128)S(1)} %copy-done.9, ...), kind=kLoop, calls=%fused_computation.29 | loop fusion | flops 8912384 | bytes 10490880 | tf_op jit(solution)/shard_map/reduce_sum | solution.py:192
  (102 shorter events, 10.5 us)
Async XLA Ops:
  0.6 26.5 %copy-start = (bf16[1,2048,176]{1,2,0:T(8,128)(2,1)S(1)}, bf16[1,2048,176]{1,2,0:T(8,128)(2,1)}, u32[]{:S(2)}) copy-start(bf16[1,2048,176]{1,2,0:T(8,128)(2,1)} %param.18) | copy-start | bytes 2162692
  0.6 8.7 %copy-start.8 = (bf16[128,2048]{1,0:T(8,128)(2,1)S(1)}, bf16[128,2048]{1,0:T(8,128)(2,1)}, u32[]{:S(2)}) copy-start(bf16[128,2048]{1,0:T(8,128)(2,1)} %param.14) | copy-start | bytes 1572868
  3.3 10.6 %copy-start.10 = (s32[128,4]{0,1:T(4,128)S(1)}, s32[128,4]{0,1:T(4,128)}, u32[]{:S(2)}) copy-start(s32[128,4]{0,1:T(4,128)} %param.16) | copy-start | bytes 6148
  3.3 18.7 %collective-permute-start = (bf16[1,1,2,16,2048]{4,3,2,1,0:T(8,128)(2,1)S(1)}, bf16[1,1,2,16,2048]{4,3,2,1,0:T(8,128)(2,1)}, u32[]{:S(2)}, u32[]{:S(2)}) collective-permute-start(bf16[1,1,2,16,2048]{4,3,2,1,0:T(8,128)(2,1)S(1)} %bitcast.132), channel_id=1, source_target_pairs={{0,1},{1,2},{2,3},{3,0},{4,5},{5,6},{6,7},{7,4},{8,9},{9,10},{10,1... | collective-permute-start | bytes 393224 | tf_op jit(solution)/shard_map/ppermute | solution.py:158
  3.9 19.2 %collective-permute-start.1 = (bf16[1,1,2,16,2048]{4,3,2,1,0:T(8,128)(2,1)S(1)}, bf16[1,1,2,16,2048]{4,3,2,1,0:T(8,128)(2,1)}, u32[]{:S(2)}, u32[]{:S(2)}) collective-permute-start(bf16[1,1,2,16,2048]{4,3,2,1,0:T(8,128)(2,1)S(1)} %bitcast.133), channel_id=1, source_target_pairs={{0,2},{1,3},{2,0},{3,1},{4,6},{5,7},{6,4},{7,5},{8,10},{9,11},{10,... | collective-permute-start | bytes 393224 | tf_op jit(solution)/shard_map/ppermute | solution.py:158
  6.4 17.6 %collective-permute-start.2 = (bf16[1,1,2,16,2048]{4,3,2,1,0:T(8,128)(2,1)S(1)}, bf16[1,1,2,16,2048]{4,3,2,1,0:T(8,128)(2,1)}, u32[]{:S(2)}, u32[]{:S(2)}) collective-permute-start(bf16[1,1,2,16,2048]{4,3,2,1,0:T(8,128)(2,1)S(1)} %bitcast.134), channel_id=1, source_target_pairs={{0,3},{1,0},{2,1},{3,2},{4,7},{5,4},{6,5},{7,6},{8,11},{9,8},{10,9... | collective-permute-start | bytes 393224 | tf_op jit(solution)/shard_map/ppermute | solution.py:158
  7.8 27.9 %collective-permute-start.3 = (bf16[1,8,37984]{2,1,0:T(8,128)(2,1)}, bf16[1,8,37984]{2,1,0:T(8,128)(2,1)S(1)}, u32[]{:S(2)}, u32[]{:S(2)}) collective-permute-start(bf16[1,8,37984]{2,1,0:T(8,128)(2,1)} %param.22), channel_id=1, source_target_pairs={{0,4},{4,8},{8,12},{12,16},{16,20},{20,24},{24,28},{28,0},{1,5},{5... | collective-permute-start | bytes 1823240 | tf_op jit(solution)/shard_map/ppermute | solution.py:34
  10.4 16.7 %all-to-all-start = ((bf16[4,2,16,2048]{3,2,1,0:T(8,128)(2,1)}), bf16[4,2,16,2048]{3,2,1,0:T(8,128)(2,1)S(1)}, u32[]{:S(2)}, u32[]{:S(2)}) async-start(bf16[4,2,16,2048]{3,2,1,0:T(8,128)(2,1)} %broadcast_in_dim.65), calls=%async_computation | async-start | bytes 1048576 | tf_op jit(solution)/shard_map/all_to_all | solution.py:151
  14.1 3.7 %copy-start.1 = (bf16[1,8,37984]{2,1,0:T(8,128)(2,1)S(1)}, bf16[1,8,37984]{2,1,0:T(8,128)(2,1)}, u32[]{:S(2)}) copy-start(bf16[1,8,37984]{2,1,0:T(8,128)(2,1)} %param.21) | copy-start | bytes 1823236
  14.1 4.1 %copy-start.13 = (u32[32]{0:T(128)S(1)}, u32[32]{0:T(128)}, u32[]{:S(2)}) copy-start(u32[32]{0:T(128)} %constant.149) | copy-start | bytes 388
  14.2 5.5 %copy-start.5 = (bf16[128,2048]{1,0:T(8,128)(2,1)S(1)}, bf16[128,2048]{1,0:T(8,128)(2,1)}, u32[]{:S(2)}) copy-start(bf16[128,2048]{1,0:T(8,128)(2,1)} %param.15) | copy-start | bytes 1572868
  17.6 3.2 %copy-start.11 = (f32[128,4]{0,1:T(4,128)S(1)}, f32[128,4]{0,1:T(4,128)}, u32[]{:S(2)}) copy-start(f32[128,4]{0,1:T(4,128)} %param.17) | copy-start | bytes 6148
  24.9 2.6 %copy-start.3 = (bf16[1,2048,176]{1,2,0:T(8,128)(2,1)S(1)}, bf16[1,2048,176]{1,2,0:T(8,128)(2,1)}, u32[]{:S(2)}) copy-start(bf16[1,2048,176]{1,2,0:T(8,128)(2,1)} %param.19) | copy-start | bytes 2162692
  27.1 1.5 %copy-start.6 = (f32[128,176]{0,1:T(8,128)S(1)}, f32[128,176]{0,1:T(8,128)}, u32[]{:S(2)}) copy-start(f32[128,176]{0,1:T(8,128)} %fusion.35) | copy-start | bytes 270340
  27.9 0.6 copy-start.7
  30.1 3.6 %copy-start.4 = (bf16[1,176,2048]{2,1,0:T(8,128)(2,1)S(1)}, bf16[1,176,2048]{2,1,0:T(8,128)(2,1)}, u32[]{:S(2)}) copy-start(bf16[1,176,2048]{2,1,0:T(8,128)(2,1)} %param.20) | copy-start | bytes 2162692
  30.1 16.9 %all-to-all-start.2 = ((bf16[4,2,16,2048]{3,2,1,0:T(8,128)(2,1)}), bf16[4,2,16,2048]{3,2,1,0:T(8,128)(2,1)S(1)}, u32[]{:S(2)}, u32[]{:S(2)}) async-start(bf16[4,2,16,2048]{3,2,1,0:T(8,128)(2,1)} %bitcast.20), calls=%async_computation.2 | async-start | bytes 1048576 | tf_op jit(solution)/shard_map/all_to_all | solution.py:169
  33.7 2.6 %copy-start.12 = (s32[1,8]{1,0:T(1,128)S(1)}, s32[1,8]{1,0:T(1,128)}, u32[]{:S(2)}) copy-start(s32[1,8]{1,0:T(1,128)} %param.23) | copy-start | bytes 100
  47.0 14.0 %all-to-all-start.1 = ((bf16[4,2,16,2048]{3,2,1,0:T(8,128)(2,1)}), bf16[4,2,16,2048]{3,2,1,0:T(8,128)(2,1)S(1)}, u32[]{:S(2)}, u32[]{:S(2)}) async-start(bf16[4,2,16,2048]{3,2,1,0:T(8,128)(2,1)} %bitcast.130), calls=%async_computation.1 | async-start | bytes 1048576 | tf_op jit(solution)/shard_map/all_to_all | solution.py:168
  64.6 5.3 %copy-start.2 = (f32[128,2048]{1,0:T(8,128)S(1)}, f32[128,2048]{1,0:T(8,128)}, u32[]{:S(2)}) copy-start(f32[128,2048]{1,0:T(8,128)} %convert_element_type.89) | copy-start | bytes 3145732
  64.6 5.3 %copy-start.9 = (f32[128,4]{1,0:T(8,128)S(1)}, f32[128,4]{1,0:T(8,128)}, u32[]{:S(2)}) copy-start(f32[128,4]{1,0:T(8,128)} %copy.40) | copy-start | bytes 6148
